TPU v7x, 32 devices: a whole 2x2x4 slice. The times are simulated.
32 devices in a mesh: dp: 16 (over z, x, core), tensor: 2 (over y).
Axes of the slice: x: 2, y: 2, z: 4, core: 2. Of those that a mesh axis runs over, the one named last changes fastest.
Arguments:
- inputs: bfloat16 [16384, 768], P(('dp', 'tensor')), may hold values from -6 to 6
- grad_out: bfloat16 [16384, 768], P(('dp', 'tensor')), may hold values from -6 to 6
- page_lengths: int32 [16, 6], P('dp'), may hold values from 0 to 1024, as said below
- gain_one: bfloat16 [768], replicated, may hold values from 0.5 to 1.5
- gain_two: bfloat16 [768], replicated, may hold values from 0.5 to 1.5
- w_query: bfloat16 [768, 768], P(None, 'tensor'), may hold values from -0.21875 to 0.21875
- w_key: bfloat16 [768, 768], P(None, 'tensor'), may hold values from -0.21875 to 0.21875
- w_value: bfloat16 [768, 768], P(None, 'tensor'), may hold values from -0.21875 to 0.21875
- w_out: bfloat16 [768, 768], P('tensor'), may hold values from -3.5 to 3.5
- w_up: bfloat16 [768, 3072], P(None, 'tensor'), may hold values from -0.21875 to 0.21875
- w_down: bfloat16 [3072, 768], P('tensor'), may hold values from -0.109375 to 0.109375
- rel_table: bfloat16 [12, 16], P('tensor'), may hold values from -4 to 4
Outputs:
- out: bfloat16 [16384, 768], P(('dp', 'tensor'))
- input_grad: bfloat16 [16384, 768], P(('dp', 'tensor'))
- gain_one_grad: float32 [768], replicated
- gain_two_grad: float32 [768], replicated
- query_grad: float32 [768, 768], P(None, 'tensor')
- key_grad: float32 [768, 768], P(None, 'tensor')
- value_grad: float32 [768, 768], P(None, 'tensor')
- out_proj_grad: float32 [768, 768], P('tensor')
- up_grad: float32 [768, 3072], P(None, 'tensor')
- down_grad: float32 [3072, 768], P('tensor')
- table_grad: float32 [12, 16], P('tensor')
Inputs may be any that keep to these rules, and one draw needn't show every extreme that they name: `page_lengths`: each row of a group lists pages of one resolution, all of 196, all of 576 or all of 1024 patches, as many as fit in 1024, then one slot with the remaining patches (possibly 0), then zeros; each row sums to 1024, and some group holds pages of 1024.
All inputs are finite; a program needn't handle non-finite values.
Results may differ from a plain program's by a relative error of at most 0.017.
Values may be sent and summed in bfloat16 or wider, within the bound.
No kernel may reach another device: no remote copies, remote signals or barrier semaphores. Data moves between devices by JAX's collectives and lax.ppermute only.
A program may use at most 192 MiB of HBM per device.

v0:
```python
import jax
import jax.numpy as jnp
from jax import lax
from jax.sharding import PartitionSpec as P

HEAD_DIM = 64
BLOCK = 512
BUCKETS = 16


def layer_norm(values, gain):
    centred = values - jnp.mean(values, axis=-1, keepdims=True)
    variance = jnp.mean(centred * centred, axis=-1, keepdims=True)
    return centred * lax.rsqrt(variance + 1e-05) * gain


def gelu_tanh(values):
    return jax.nn.gelu(values, approximate=True)


def plain_times(left_side, right_side):
    return jnp.dot(left_side, right_side, preferred_element_type=jnp.float32)


def times_transposed(left_side, right_side):
    return lax.dot_general(
        left_side, right_side, (((1,), (1,)), ((), ())), preferred_element_type=jnp.float32
    )


def transposed_times(left_side, right_side):
    return lax.dot_general(
        left_side, right_side, (((0,), (0,)), ((), ())), preferred_element_type=jnp.float32
    )


def relative(first_row, key_count):
    half_count = BUCKETS // 2
    row_pos = first_row + jnp.arange(BLOCK, dtype=jnp.int32)
    offsets = row_pos[:, None] - jnp.arange(key_count, dtype=jnp.int32)[None, :]
    distance = jnp.abs(offsets) + 1
    levels = jnp.zeros_like(offsets)
    for exponent in range(1, half_count):
        levels = levels + (distance >= 2**exponent).astype(jnp.int32)
    buckets = levels + half_count * (offsets < 0).astype(jnp.int32)
    return (buckets[:, :, None] == jnp.arange(BUCKETS, dtype=jnp.int32)[None, None, :]).astype(
        jnp.bfloat16
    )


def body(
    inputs,
    grad_out,
    page_lengths,
    gain_one,
    gain_two,
    w_query,
    w_key,
    w_value,
    w_out,
    w_up,
    w_down,
    rel_table,
):
    local_heads = w_query.shape[1] // HEAD_DIM
    score_scale = HEAD_DIM ** (-0.5)
    gain_first = gain_one.astype(jnp.float32)
    gain_second = gain_two.astype(jnp.float32)
    tokens = inputs.astype(jnp.float32)
    normed_own = layer_norm(tokens, gain_first).astype(jnp.bfloat16)
    normed = lax.all_gather(normed_own, "tensor", axis=0, tiled=True)
    group_rows = normed.shape[0]
    heads_view = (group_rows, local_heads, HEAD_DIM)
    query_heads = plain_times(normed, w_query).astype(jnp.bfloat16).reshape(heads_view)
    key_heads = plain_times(normed, w_key).astype(jnp.bfloat16).reshape(heads_view)
    value_heads = plain_times(normed, w_value).astype(jnp.bfloat16).reshape(heads_view)
    page_ends = jnp.cumsum(page_lengths[0])
    positions = jnp.arange(group_rows, dtype=jnp.int32)
    page_of = jnp.sum((positions[:, None] >= page_ends[None, :]).astype(jnp.int32), axis=1)

    def block_scores(first_row):
        query_block = lax.dynamic_slice_in_dim(query_heads, first_row, BLOCK, 0)
        raw_scores = (
            jnp.einsum("qhd,khd->hqk", query_block, key_heads, preferred_element_type=jnp.float32)
            * score_scale
        )
        one_hot = relative(first_row, group_rows)
        bias = jnp.einsum("qkm,hm->hqk", one_hot, rel_table, preferred_element_type=jnp.float32)
        scores = raw_scores + bias
        same_page = (
            lax.dynamic_slice_in_dim(page_of, first_row, BLOCK, 0)[:, None] == page_of[None, :]
        )
        scores = jnp.where(same_page[None], scores, -1e30)
        return (query_block, scores, one_hot)

    def attend(first_row):
        scores = block_scores(first_row)[1]
        log_total = jax.nn.logsumexp(scores, axis=-1)
        weight = jnp.exp(scores - log_total[..., None]).astype(jnp.bfloat16)
        block_out = jnp.einsum(
            "hqk,khd->qhd", weight, value_heads, preferred_element_type=jnp.float32
        )
        return (block_out.astype(jnp.bfloat16), log_total)

    starts = jnp.arange(group_rows // BLOCK, dtype=jnp.int32) * BLOCK
    attended_blocks, log_totals = lax.map(attend, starts)
    attended = attended_blocks.reshape(group_rows, local_heads * HEAD_DIM)
    branch_one = lax.psum_scatter(
        plain_times(attended, w_out), "tensor", scatter_dimension=0, tiled=True
    )
    middle = tokens + branch_one
    normed_two_own = layer_norm(middle, gain_second).astype(jnp.bfloat16)
    normed_two = lax.all_gather(normed_two_own, "tensor", axis=0, tiled=True)
    up_use, down_use = (w_up, w_down)
    pre_act = plain_times(normed_two, up_use)
    hidden = gelu_tanh(pre_act).astype(jnp.bfloat16)
    branch_two = lax.psum_scatter(
        plain_times(hidden, down_use).astype(jnp.bfloat16),
        "tensor",
        scatter_dimension=0,
        tiled=True,
    ).astype(jnp.float32)
    grad_rows = lax.all_gather(grad_out, "tensor", axis=0, tiled=True)
    out = (middle + branch_two).astype(jnp.bfloat16)
    down_part = transposed_times(hidden, grad_rows)
    grad_hidden = times_transposed(grad_rows, down_use)
    gelu_back = jax.vjp(gelu_tanh, pre_act)[1]
    grad_pre = gelu_back(grad_hidden)[0].astype(jnp.bfloat16)
    up_part = transposed_times(normed_two, grad_pre)
    grad_normed_two = lax.psum_scatter(
        times_transposed(grad_pre, w_up).astype(jnp.bfloat16),
        "tensor",
        scatter_dimension=0,
        tiled=True,
    ).astype(jnp.float32)
    up_final, down_final = (up_part, down_part)
    norm_two_back = jax.vjp(layer_norm, middle, gain_second)[1]
    grad_middle_norm, gain_two_part = norm_two_back(grad_normed_two)
    grad_middle = grad_out.astype(jnp.float32) + grad_middle_norm
    grad_branch = lax.all_gather(grad_middle.astype(jnp.bfloat16), "tensor", axis=0, tiled=True)
    out_proj_grad = transposed_times(attended, grad_branch)
    grad_attended = times_transposed(grad_branch, w_out).astype(jnp.bfloat16).reshape(heads_view)

    def attend_back(carry, block_pair):
        key_acc, value_acc, table_acc = carry
        first_row, log_total = block_pair
        query_block, scores, one_hot = block_scores(first_row)
        prob = jnp.exp(scores - log_total[..., None])
        prob_low = prob.astype(jnp.bfloat16)
        grad_block = lax.dynamic_slice_in_dim(grad_attended, first_row, BLOCK, 0)
        grad_prob = jnp.einsum(
            "qhd,khd->hqk", grad_block, value_heads, preferred_element_type=jnp.float32
        )
        row_inner = jnp.sum(prob * grad_prob, axis=-1, keepdims=True)
        grad_scores = prob * (grad_prob - row_inner)
        table_step = jnp.einsum(
            "hqk,qkm->hm", grad_scores, one_hot.astype(jnp.float32), precision=lax.Precision.HIGH
        )
        scores_low = grad_scores.astype(jnp.bfloat16)
        grad_query = (
            jnp.einsum("hqk,khd->qhd", scores_low, key_heads, preferred_element_type=jnp.float32)
            * score_scale
        )
        key_acc = (
            key_acc
            + jnp.einsum(
                "hqk,qhd->khd", scores_low, query_block, preferred_element_type=jnp.float32
            )
            * score_scale
        )
        value_acc = value_acc + jnp.einsum(
            "hqk,qhd->khd", prob_low, grad_block, preferred_element_type=jnp.float32
        )
        table_acc = table_acc + table_step
        return ((key_acc, value_acc, table_acc), grad_query.astype(jnp.bfloat16))

    zero_heads = jnp.zeros(heads_view, jnp.float32)
    zero_table = jnp.zeros((local_heads, BUCKETS), jnp.float32)
    (key_sum, value_sum, table_part), query_blocks = lax.scan(
        attend_back, (zero_heads, zero_heads, zero_table), (starts, log_totals)
    )
    flat_width = local_heads * HEAD_DIM
    grad_query = query_blocks.reshape(group_rows, flat_width)
    grad_key = key_sum.astype(jnp.bfloat16).reshape(group_rows, flat_width)
    grad_value = value_sum.astype(jnp.bfloat16).reshape(group_rows, flat_width)
    query_part = transposed_times(normed, grad_query)
    key_part = transposed_times(normed, grad_key)
    value_part = transposed_times(normed, grad_value)
    total = times_transposed(grad_query, w_query)
    total = total + times_transposed(grad_key, w_key)
    grad_normed_one = lax.psum_scatter(
        (total + times_transposed(grad_value, w_value)).astype(jnp.bfloat16),
        "tensor",
        scatter_dimension=0,
        tiled=True,
    ).astype(jnp.float32)
    norm_one_back = jax.vjp(layer_norm, tokens, gain_first)[1]
    grad_tokens, gain_one_part = norm_one_back(grad_normed_one)
    input_grad = (grad_middle + grad_tokens).astype(jnp.bfloat16)
    summed = lax.psum(
        (query_part, key_part, value_part, out_proj_grad, up_final, down_final, table_part), "dp"
    )
    query_total, key_total, value_total, out_total, up_total, down_total, table_total = summed
    gain_sums = lax.psum((gain_one_part, gain_two_part), ("dp", "tensor"))
    return (
        out,
        input_grad,
        gain_sums[0],
        gain_sums[1],
        query_total,
        key_total,
        value_total,
        out_total,
        up_total,
        down_total,
        table_total,
    )


def solution(mesh):
    in_specs = (
        P(("dp", "tensor"), None),
        P(("dp", "tensor"), None),
        P("dp", None),
        P(),
        P(),
        P(None, "tensor"),
        P(None, "tensor"),
        P(None, "tensor"),
        P("tensor", None),
        P(None, "tensor"),
        P("tensor", None),
        P("tensor", None),
    )
    out_specs = (
        P(("dp", "tensor"), None),
        P(("dp", "tensor"), None),
        P(),
        P(),
        P(None, "tensor"),
        P(None, "tensor"),
        P(None, "tensor"),
        P("tensor", None),
        P(None, "tensor"),
        P("tensor", None),
        P("tensor", None),
    )
    return jax.shard_map(body, mesh=mesh, in_specs=in_specs, out_specs=out_specs, check_vma=False)
```

profile of v0, /device:TPU:0, one launch (start us, length us, event | category | flops | bytes accessed | tf_op | source)
XLA Modules:
  0.0 885.2 jit_solution(784256954340176046)
XLA Ops:
  13.7 29.7 %all-gather.5.cloned.1.call-done = bf16[1024,768]{1,0:T(8,128)(2,1)} async-done(((bf16[512,768]{1,0:T(8,128)(2,1)}), bf16[1024,768]{1,0:T(8,128)(2,1)}) %all-gather.5.cloned.1.call-update) | async-done | bytes 1572880 | tf_op jit(solution)/shard_map/all_gather | solution.py:71
  43.4 3.4 convolution_convert_fusion.3
  51.4 84.2 %while.29 = (s32[]{:T(128)}, bf16[2,512,6,64]{1,3,2,0:T(8,128)(2,1)}, f32[2,6,512]{2,1,0:T(8,128)S(1)}, s32[2]{0:T(128)S(1)}, s32[1024]{0:T(1024)S(1)}, /*index=...) while((s32[]{:T(128)}, ...), condition=%wide.region_7.8_spmd, body=%wide.region_4.7_spmd.sunk | while | flops 953901568 | bytes 133609992 | solution.py:106
  57.3 8.4 fusion.175
  65.7 15.3 %fusion.176 = (f32[6,512]{1,0:T(8,128)S(1)}, f32[6,512,1024]{2,1,0:T(8,128)S(1)}) fusion(f32[512,1024,6]{1,2,0:T(8,128)} %fusion.175, bf16[1024,6,64]{0,2,1:T(8,128)(2,1)S(1)} %get-tuple-element.416, bf16[1024,6,64]{0,2,1:T(8,128)(2,1)S(1)} %copy-done.8, s32[]{:T(128)S(6)} %select_n.59, pred[512,1024]{1,0:T(8,128)(4,1)S(1)} %broadcast_compare_fusion.4), kind=kOutput, calls=%fused_computation.146.clone.1 | convolution fusion | flops 415233024 | bytes 26882052 | tf_op jit(solution)/shard_map/while/body/eval_jaxpr/qhd,khd->hqk/dot_general | solution.py:84
  81.1 2.8 exponential_reduce_fusion.2
  85.8 6.7 fusion.178
  99.1 8.4 fusion.175
  107.5 15.3 %fusion.176 = (f32[6,512]{1,0:T(8,128)S(1)}, f32[6,512,1024]{2,1,0:T(8,128)S(1)}) fusion(f32[512,1024,6]{1,2,0:T(8,128)} %fusion.175, bf16[1024,6,64]{0,2,1:T(8,128)(2,1)S(1)} %get-tuple-element.416, bf16[1024,6,64]{0,2,1:T(8,128)(2,1)S(1)} %copy-done.8, s32[]{:T(128)S(6)} %select_n.59, pred[512,1024]{1,0:T(8,128)(4,1)S(1)} %broadcast_compare_fusion.4), kind=kOutput, calls=%fused_computation.146.clone.1 | convolution fusion | flops 415233024 | bytes 26882052 | tf_op jit(solution)/shard_map/while/body/eval_jaxpr/qhd,khd->hqk/dot_general | solution.py:84
  127.6 6.7 fusion.178
  142.2 42.7 %reduce-scatter.5.cloned.1.call-done = f32[512,768]{1,0:T(8,128)} async-done(((f32[1024,768]{1,0:T(8,128)}), f32[512,768]{1,0:T(8,128)}) %reduce-scatter.5.cloned.1.call-update) | async-done | bytes 1572880 | tf_op jit(solution)/shard_map/reduce_scatter | solution.py:108
  189.1 24.7 %all-gather.9.cloned.1.call-done = bf16[1024,768]{1,0:T(8,128)(2,1)} async-done(((bf16[512,768]{1,0:T(8,128)(2,1)}), bf16[1024,768]{1,0:T(8,128)(2,1)}) %all-gather.9.cloned.1.call-update) | async-done | bytes 1572880 | tf_op jit(solution)/shard_map/all_gather | solution.py:123
  213.8 7.5 fusion.101
  221.2 21.8 %all-gather.7.cloned.1.call-done = bf16[1024,768]{1,0:T(8,128)(2,1)} async-done(((bf16[512,768]{1,0:T(8,128)(2,1)}), bf16[1024,768]{1,0:T(8,128)(2,1)}) %all-gather.7.cloned.1.call-update) | async-done | bytes 1572880 | tf_op jit(solution)/shard_map/all_gather | solution.py:113
  243.1 9.7 %fusion.77 = (bf16[1024,1536]{1,0:T(8,128)(2,1)S(1)}, f32[1024,1536]{1,0:T(8,128)}) fusion(f32[1024,1536]{1,0:T(8,128)} %fusion.101, bf16[1024,768]{1,0:T(8,128)(2,1)} %all-gather.7.cloned.1.call-done, bf16[768,1536]{1,0:T(8,128)(2,1)S(1)} %copy-done), kind=kOutput, calls=%fused_computation.91 | convolution fusion | flops 2447376384 | bytes 19660800 | tf_op jit(solution)/shard_map/dot_general | solution.py:22
  254.4 3.7 convolution_convert_fusion
  258.2 8.4 convolution_convert_fusion.1
  266.7 17.7 %reduce-scatter.9.cloned.1.call-done = bf16[512,768]{1,0:T(8,128)(2,1)} async-done(((bf16[1024,768]{1,0:T(8,128)(2,1)}), bf16[512,768]{1,0:T(8,128)(2,1)}) %reduce-scatter.9.cloned.1.call-update) | async-done | bytes 786448 | tf_op jit(solution)/shard_map/reduce_scatter | solution.py:130
  286.9 25.8 %reduce-scatter.7.cloned.1.call-done = bf16[512,768]{1,0:T(8,128)(2,1)} async-done(((bf16[1024,768]{1,0:T(8,128)(2,1)}), bf16[512,768]{1,0:T(8,128)(2,1)}) %reduce-scatter.7.cloned.1.call-update) | async-done | bytes 786448 | tf_op jit(solution)/shard_map/reduce_scatter | solution.py:117
  312.6 2.9 fusion.97
  318.0 27.3 %all-gather.11.cloned.1.call-done = bf16[1024,768]{1,0:T(8,128)(2,1)} async-done(((bf16[512,768]{1,0:T(8,128)(2,1)}), bf16[1024,768]{1,0:T(8,128)(2,1)}) %all-gather.11.cloned.1.call-update) | async-done | bytes 1572880 | tf_op jit(solution)/shard_map/all_gather | solution.py:140
  345.2 3.1 convolution_convert_fusion.2
  349.3 214.7 %while.30 = (s32[]{:T(128)}, f32[1024,6,64]{0,2,1:T(8,128)}, f32[1024,6,64]{0,2,1:T(8,128)}, f32[6,16]{1,0:T(8,128)S(1)}, bf16[2,512,6,64]{1,3,2,0:T(8,128)(2,1)...) while((s32[]{:T(128)}, f32[1024,6,64]{0,2,1:T(8,128)}, ...), condition=%wide.region_17.18_spmd.clone, body=%wide.region_15.17_spmd.clone.sunk | while | flops 2483812096 | bytes 329461056 | solution.py:179
  356.3 6.4 fusion.191
  362.7 8.5 fusion.192
  371.2 15.7 %copy.43 = f32[512,1024,6]{1,0,2:T(8,128)} copy(f32[512,1024,6]{0,2,1:T(8,128)} %fusion.192) | data formatting | bytes 25165824 | tf_op jit(solution)/shard_map/while/body/eval_jaxpr/qkm,hm->hqk/dot_general | solution.py:88
  386.9 13.8 %multiply_reduce_fusion.3 = (f32[6,512]{1,0:T(8,128)S(1)}, f32[6,512,1024]{2,1,0:T(8,128)}) fusion(f32[6,512,1024]{2,1,0:T(8,128)} %fusion.191, f32[6,512]{1,0:T(8,128)S(1)} %dynamic-slice_bitcast_fusion.2, f32[512,1024,6]{1,0,2:T(8,128)} %copy.43, bf16[1024,6,64]{0,2,1:T(8,128)(2,1)S(1)} %get-tuple-element.462, ...), kind=kOutput, calls=%fused_computation.44.clone.1 | convolution fusion | flops 421524480 | bytes 39477252 | tf_op jit(solution)/shard_map/while/body/eval_jaxpr/qhd,khd->hqk/dot_general | solution.py:84
  400.7 9.1 %subtract_multiply_fusion.2 = f32[6,512,1024]{2,1,0:T(8,128)S(1)} fusion(f32[6,512,1024]{2,1,0:T(8,128)} %get-tuple-element.384, f32[6,512,1024]{2,1,0:T(8,128)} %fusion.191, f32[6,512]{1,0:T(8,128)S(1)} %get-tuple-element.385), kind=kLoop, calls=%fused_computation.43.clone.1 | loop fusion | flops 6291456 | bytes 37761024 | tf_op jit(solution)/shard_map/while/body/eval_jaxpr/mul | solution.py:155
  412.6 3.0 bitcast_add_fusion.7
  415.6 2.8 fusion.194
  418.4 3.5 bitcast_add_fusion.6
  422.0 16.0 %copy.44 = f32[6,512,1024]{1,0,2:T(8,128)} copy(f32[6,512,1024]{2,1,0:T(8,128)} %copy-done.2) | data formatting | bytes 25165824 | tf_op jit(solution)/shard_map/while/body/eval_jaxpr/mul | solution.py:155
  437.9 17.4 %fusion.193 = f32[6,16]{1,0:T(8,128)S(1)} fusion(f32[6,512,1024]{1,0,2:T(8,128)} %copy.44, s32[512,1024]{0,1:T(8,128)S(1)} %select_add_fusion.5, f32[6,16]{1,0:T(8,128)S(1)} %get-tuple-element.441, pred[]{:T(512)S(6)} %compare.3), kind=kOutput, calls=%fused_computation.69.clone.1 | convolution fusion | flops 310378688 | bytes 14680833 | tf_op jit(solution)/shard_map/while/body/eval_jaxpr/hqk,qkm->hm/dot_general | solution.py:156
  462.2 6.5 fusion.191
  468.6 8.5 fusion.192
  477.1 15.7 %copy.43 = f32[512,1024,6]{1,0,2:T(8,128)} copy(f32[512,1024,6]{0,2,1:T(8,128)} %fusion.192) | data formatting | bytes 25165824 | tf_op jit(solution)/shard_map/while/body/eval_jaxpr/qkm,hm->hqk/dot_general | solution.py:88
  492.8 13.8 %multiply_reduce_fusion.3 = (f32[6,512]{1,0:T(8,128)S(1)}, f32[6,512,1024]{2,1,0:T(8,128)}) fusion(f32[6,512,1024]{2,1,0:T(8,128)} %fusion.191, f32[6,512]{1,0:T(8,128)S(1)} %dynamic-slice_bitcast_fusion.2, f32[512,1024,6]{1,0,2:T(8,128)} %copy.43, bf16[1024,6,64]{0,2,1:T(8,128)(2,1)S(1)} %get-tuple-element.462, ...), kind=kOutput, calls=%fused_computation.44.clone.1 | convolution fusion | flops 421524480 | bytes 39477252 | tf_op jit(solution)/shard_map/while/body/eval_jaxpr/qhd,khd->hqk/dot_general | solution.py:84
  506.6 9.1 %subtract_multiply_fusion.2 = f32[6,512,1024]{2,1,0:T(8,128)S(1)} fusion(f32[6,512,1024]{2,1,0:T(8,128)} %get-tuple-element.384, f32[6,512,1024]{2,1,0:T(8,128)} %fusion.191, f32[6,512]{1,0:T(8,128)S(1)} %get-tuple-element.385), kind=kLoop, calls=%fused_computation.43.clone.1 | loop fusion | flops 6291456 | bytes 37761024 | tf_op jit(solution)/shard_map/while/body/eval_jaxpr/mul | solution.py:155
  518.5 5.0 bitcast_add_fusion.7
  523.6 2.8 fusion.194
  526.4 4.0 bitcast_add_fusion.6
  530.4 16.0 %copy.44 = f32[6,512,1024]{1,0,2:T(8,128)} copy(f32[6,512,1024]{2,1,0:T(8,128)} %copy-done.2) | data formatting | bytes 25165824 | tf_op jit(solution)/shard_map/while/body/eval_jaxpr/mul | solution.py:155
  546.4 17.4 %fusion.193 = f32[6,16]{1,0:T(8,128)S(1)} fusion(f32[6,512,1024]{1,0,2:T(8,128)} %copy.44, s32[512,1024]{0,1:T(8,128)S(1)} %select_add_fusion.5, f32[6,16]{1,0:T(8,128)S(1)} %get-tuple-element.441, pred[]{:T(512)S(6)} %compare.3), kind=kOutput, calls=%fused_computation.69.clone.1 | convolution fusion | flops 310378688 | bytes 14680833 | tf_op jit(solution)/shard_map/while/body/eval_jaxpr/hqk,qkm->hm/dot_general | solution.py:156
  572.4 7.3 fusion.108
  579.7 8.8 fusion.96
  596.5 35.2 %psum.71 = f32[6,16]{1,0:T(8,128)} all-reduce(f32[6,16]{1,0:T(8,128)S(1)} %get-tuple-element.134), channel_id=1, replica_groups=mesh['dp'=16,'tensor'=2] {'dp'}, use_global_device_ids=true, to_apply=%region_31.32 | all-reduce | flops 96 | bytes 768 | tf_op jit(solution)/shard_map/psum | solution.py:200
  635.4 38.2 %all-reduce = (f32[768]{0:T(1024)}, f32[768]{0:T(1024)}) all-reduce(f32[768]{0:T(1024)S(1)} %get-tuple-element.179, f32[768]{0:T(1024)S(1)} %copy-done.45), channel_id=1, replica_groups=mesh['dp'=16,'tensor'=2] {'dp','tensor'}, use_global_device_ids=true, to_apply=%region_22.23 | all-reduce | flops 1536 | bytes 12288 | tf_op jit(solution)/shard_map/psum | solution.py:204
  676.4 189.9 %all-reduce.4.cloned.1.call-done = (f32[768,384]{1,0:T(8,128)}, f32[768,384]{1,0:T(8,128)}, f32[768,384]{1,0:T(8,128)}, f32[384,768]{1,0:T(8,128)}, f32[768,1536]{1,0:T(8,128)}, /*index=5*/f32[1536,768]{1,0:T(8,128)}) async-done(((f32[768,384]{1,0:T(8,128)}, f32[768,384]{1,0:T(8,128)}, f32[768,384]{1,0:T(8,128)}, f32[384,768]{1,0:T(8,128)}, f32[768,1536]{1,0:T(8,128)}, /*index=5*/f32[1536,768]{1,0:T(8,128)}), ...) | async-done | bytes 14155792 | tf_op jit(solution)/shard_map/psum | solution.py:200
  (229 shorter events, 94.7 us)
Async XLA Ops:
  7.2 235.9 %copy-start = (bf16[768,1536]{1,0:T(8,128)(2,1)S(1)}, bf16[768,1536]{1,0:T(8,128)(2,1)}, u32[]{:S(2)}) copy-start(bf16[768,1536]{1,0:T(8,128)(2,1)} %param.25) | copy-start | bytes 7077892
  7.2 4.9 copy-start.11
  7.2 6.2 copy-start.51
  7.2 36.2 %all-gather.5.cloned.1.call-start = ((), (), s32[]{:S(2)}) async-start(), calls=%async_computation.4 | async-start | bytes 2359296 | tf_op jit(solution)/shard_map/all_gather | solution.py:71
  13.3 171.6 %reduce-scatter.5.cloned.1.call-start = ((), (), s32[]{:S(2)}) async-start(), calls=%async_computation.5 | async-start | bytes 4718592 | tf_op jit(solution)/shard_map/reduce_scatter | solution.py:108
  57.3 8.4 copy-start.8
  81.0 4.7 copy-start.3
  81.1 4.7 copy-start.5
  81.1 4.7 copy-start.20
  99.1 8.4 copy-start.8
  122.8 4.7 copy-start.3
  122.8 4.7 copy-start.5
  122.8 4.7 copy-start.20
  141.4 72.4 %all-gather.9.cloned.1.call-start = ((), (), s32[]{:S(2)}) async-start(), calls=%async_computation.8 | async-start | bytes 2359296 | tf_op jit(solution)/shard_map/all_gather | solution.py:123
  142.1 100.9 %all-gather.7.cloned.1.call-start = ((), (), s32[]{:S(2)}) async-start(), calls=%async_computation.6 | async-start | bytes 2359296 | tf_op jit(solution)/shard_map/all_gather | solution.py:113
  189.0 95.4 %reduce-scatter.9.cloned.1.call-start = ((), (), s32[]{:S(2)}) async-start(), calls=%async_computation.9 | async-start | bytes 2359296 | tf_op jit(solution)/shard_map/reduce_scatter | solution.py:130
  258.2 54.5 %reduce-scatter.7.cloned.1.call-start = ((), (), s32[]{:S(2)}) async-start(), calls=%async_computation.7 | async-start | bytes 2359296 | tf_op jit(solution)/shard_map/reduce_scatter | solution.py:117
  266.7 17.8 %copy-start.10 = (f32[512,768]{1,0:T(8,128)S(1)}, f32[512,768]{1,0:T(8,128)}, u32[]{:S(2)}) copy-start(f32[512,768]{1,0:T(8,128)} %copy-done.9) | copy-start | bytes 4718596
  266.7 78.6 %all-gather.11.cloned.1.call-start = ((), (), s32[]{:S(2)}) async-start(), calls=%async_computation.10 | async-start | bytes 2359296 | tf_op jit(solution)/shard_map/all_gather | solution.py:140
  286.9 29.8 %copy-start.17 = (bf16[512,768]{1,0:T(8,128)(2,1)S(1)}, bf16[512,768]{1,0:T(8,128)(2,1)}, u32[]{:S(2)}) copy-start(bf16[512,768]{1,0:T(8,128)(2,1)} %param.17) | copy-start | bytes 2359300
  315.6 29.7 %copy-start.29 = (bf16[384,768]{1,0:T(8,128)(2,1)S(1)}, bf16[384,768]{1,0:T(8,128)(2,1)}, u32[]{:S(2)}) copy-start(bf16[384,768]{1,0:T(8,128)(2,1)} %param.24) | copy-start | bytes 1769476
  315.6 32.8 %copy-start.41 = (f32[512]{0:T(512)}, f32[512]{0:T(512)S(1)}, u32[]{:S(2)}) copy-start(f32[512]{0:T(512)S(1)} %negate_multiply_fusion.1) | copy-start | bytes 6148
  317.9 313.8 %reduce-scatter.11.cloned.1.call-start = ((), (), s32[]{:S(2)}) async-start(), calls=%async_computation.11 | async-start | bytes 2359296 | tf_op jit(solution)/shard_map/reduce_scatter | solution.py:191
  352.2 4.0 copy-start.6
  352.2 4.0 copy-start.13
  400.7 11.8 %copy-start.4 = (f32[6,512,1024]{2,1,0:T(8,128)S(1)}, f32[6,512,1024]{2,1,0:T(8,128)}, u32[]{:S(2)}) copy-start(f32[6,512,1024]{2,1,0:T(8,128)} %get-tuple-element.384) | copy-start | bytes 37748740 | tf_op jit(solution)/shard_map/while
  400.7 11.9 %copy-start.14 = (bf16[1024,6,64]{0,2,1:T(8,128)(2,1)S(1)}, bf16[1024,6,64]{0,2,1:T(8,128)(2,1)}, u32[]{:S(2)}) copy-start(bf16[1024,6,64]{0,2,1:T(8,128)(2,1)} %get-tuple-element.465) | copy-start | bytes 2359300 | tf_op jit(solution)/shard_map/while
  412.6 5.8 copy-start.2
  458.1 4.0 copy-start.6
  458.1 4.0 copy-start.13
  506.6 11.8 %copy-start.4 = (f32[6,512,1024]{2,1,0:T(8,128)S(1)}, f32[6,512,1024]{2,1,0:T(8,128)}, u32[]{:S(2)}) copy-start(f32[6,512,1024]{2,1,0:T(8,128)} %get-tuple-element.384) | copy-start | bytes 37748740 | tf_op jit(solution)/shard_map/while
  506.6 11.9 %copy-start.14 = (bf16[1024,6,64]{0,2,1:T(8,128)(2,1)S(1)}, bf16[1024,6,64]{0,2,1:T(8,128)(2,1)}, u32[]{:S(2)}) copy-start(bf16[1024,6,64]{0,2,1:T(8,128)(2,1)} %get-tuple-element.465) | copy-start | bytes 2359300 | tf_op jit(solution)/shard_map/while
  518.5 7.9 copy-start.2
  572.3 294.0 %all-reduce.4.cloned.1.call-start = ((), (), s32[]{:S(2)}) async-start(), calls=%async_computation.12 | async-start | bytes 28311552 | tf_op jit(solution)/shard_map/psum | solution.py:200
  572.4 7.3 copy-start.49
  579.7 8.8 copy-start.24
  579.7 8.8 copy-start.50
  596.4 35.3 %copy-start.12 = (bf16[512,768]{1,0:T(8,128)(2,1)S(1)}, bf16[512,768]{1,0:T(8,128)(2,1)}, u32[]{:S(2)}) copy-start(bf16[512,768]{1,0:T(8,128)(2,1)} %param.16) | copy-start | bytes 2359300
  596.4 35.3 %copy-start.36 = (f32[768]{0:T(1024)S(1)}, f32[768]{0:T(1024)}, u32[]{:S(2)}) copy-start(f32[768]{0:T(1024)} %copy-done.35) | copy-start | bytes 9220
  596.4 35.3 %copy-start.38 = (f32[512]{0:T(512)S(1)}, f32[512]{0:T(512)}, u32[]{:S(2)}) copy-start(f32[512]{0:T(512)} %copy-done.37) | copy-start | bytes 6148
  596.4 36.9 %copy-start.44 = (f32[512]{0:T(512)S(1)}, f32[512]{0:T(512)}, u32[]{:S(2)}) copy-start(f32[512]{0:T(512)} %copy-done.43) | copy-start | bytes 6148
  596.4 36.9 %copy-start.40 = (f32[512]{0:T(512)S(1)}, f32[512]{0:T(512)}, u32[]{:S(2)}) copy-start(f32[512]{0:T(512)} %copy-done.39) | copy-start | bytes 6148
  596.5 39.0 %copy-start.45 = (f32[768]{0:T(1024)S(1)}, f32[768]{0:T(1024)}, u32[]{:S(2)}) copy-start(f32[768]{0:T(1024)} %get-tuple-element.177) | copy-start | bytes 9220
  596.5 77.2 %copy-start.16 = (f32[512,768]{1,0:T(8,128)S(1)}, f32[512,768]{1,0:T(8,128)}, u32[]{:S(2)}) copy-start(f32[512,768]{1,0:T(8,128)} %copy-done.15) | copy-start | bytes 4718596
  596.5 77.2 %copy-start.18 = (bf16[512,768]{1,0:T(8,128)(2,1)S(1)}, bf16[512,768]{1,0:T(8,128)(2,1)}, u32[]{:S(2)}) copy-start(bf16[512,768]{1,0:T(8,128)(2,1)} %param.17) | copy-start | bytes 2359300
  596.5 77.2 %copy-start.42 = (f32[512]{0:T(512)S(1)}, f32[512]{0:T(512)}, u32[]{:S(2)}) copy-start(f32[512]{0:T(512)} %copy-done.41) | copy-start | bytes 6148
  866.3 4.5 copy-start.25
  870.9 3.8 slice-start
  (25 other events, 46.5 us)
Sparse Core Ops, SparseCore 0:
  13.4 29.8 all-gather.4
  141.5 43.3 reduce-scatter.4
  186.5 27.2 all-gather.8
  215.8 27.1 all-gather.6
  258.3 26.0 reduce-scatter.8
  286.5 26.0 reduce-scatter.6
  318.0 27.1 all-gather.10
  572.4 26.0 reduce-scatter.10
  604.8 261.4 all-reduce.3
where the time goes:
time: 891 us; the launch traced here: 885 us
  waiting for transfers between devices  380 us (43%)
  matrix products  245 us (27%)
  local copies, waits for them, and re-layouts  101 us (11%)
  blocking collectives  73.4 us (8%)
  other arithmetic  61 us (7%)
  between operations  14.6 us (2%)
  loops' own time  9.43 us (1%)
    psum x1, waiting for transfers between devices, body(): lax.psum((query_part, key_part, value_part, out_proj_grad, up_final, down...  190 us
    dot_general x4, matrix products, block_scores(): jnp.einsum('qhd,khd->hqk', query_block, key_heads, preferred_element_type...  58.2 us
    reduce_scatter x1, waiting for transfers between devices, body(): lax.psum_scatter(plain_times(attended, w_out), 'tensor', scatter_dimensio...  42.7 us
    psum x1, blocking collectives, body(): gain_sums = lax.psum((gain_one_part, gain_two_part), ('dp', 'tensor'))  38.2 us
    psum x1, blocking collectives, body(): lax.psum((query_part, key_part, value_part, out_proj_grad, up_final, down...  35.2 us
    dot_general x2, matrix products, attend_back(): jnp.einsum('hqk,qkm->hm', grad_scores, one_hot.astype(jnp.float32), preci...  34.8 us
    dot_general x4, matrix products, block_scores(): jnp.einsum('qkm,hm->hqk', one_hot, rel_table, preferred_element_type=jnp....  33.8 us
    mul x2, local copies, waits for them, and re-layouts, attend_back(): grad_scores = prob * (grad_prob - row_inner)  31.9 us
  transfers between devices with their start and end apart: 9, of which 8 were waited for; matrix products, arithmetic and copies ran while one was open for 6% of the time, Pallas kernels for 0%

commit v1 on v0

--- a/solution.py
+++ b/solution.py
@@ -201,7 +201,7 @@
         (query_part, key_part, value_part, out_proj_grad, up_final, down_final, table_part), "dp"
     )
     query_total, key_total, value_total, out_total, up_total, down_total, table_total = summed
-    gain_sums = lax.psum((gain_one_part, gain_two_part), ("dp", "tensor"))
+    gain_sums = lax.psum(lax.psum((gain_one_part, gain_two_part), "tensor"), "dp")
     return (
         out,
         input_grad,

time: 891 us -> 889 us (level)
  transfers between devices with their start and end apart: 9 -> 9, of which waited for: 8 -> 9; matrix products, arithmetic and copies ran while one was open for 6% -> 6% of each run, Pallas kernels for 0% -> 0%
where the time goes in v1:
time: 889 us; the launch traced here: 884 us
  waiting for transfers between devices  385 us (43%)
  matrix products  245 us (28%)
  local copies, waits for them, and re-layouts  101 us (11%)
  blocking collectives  68.5 us (8%)
  other arithmetic  60.8 us (7%)
  between operations  14.6 us (2%)
  loops' own time  9.03 us (1%)
    psum x1, waiting for transfers between devices, body(): lax.psum((query_part, key_part, value_part, out_proj_grad, up_final, down...  192 us
    psum x1, blocking collectives, body(): lax.psum(lax.psum((gain_one_part, gain_two_part), 'tensor'), 'dp')  63.5 us
    dot_general x4, matrix products, block_scores(): jnp.einsum('qhd,khd->hqk', query_block, key_heads, preferred_element_type...  58.3 us
    reduce_scatter x1, waiting for transfers between devices, body(): lax.psum_scatter(plain_times(attended, w_out), 'tensor', scatter_dimensio...  42.7 us
    dot_general x2, matrix products, attend_back(): jnp.einsum('hqk,qkm->hm', grad_scores, one_hot.astype(jnp.float32), preci...  34.8 us
    dot_general x4, matrix products, block_scores(): jnp.einsum('qkm,hm->hqk', one_hot, rel_table, preferred_element_type=jnp....  33.9 us
    mul x2, local copies, waits for them, and re-layouts, attend_back(): grad_scores = prob * (grad_prob - row_inner)  31.9 us
    dot_general x2, local copies, waits for them, and re-layouts, block_scores(): jnp.einsum('qkm,hm->hqk', one_hot, rel_table, preferred_element_type=jnp....  31.3 us
  transfers between devices with their start and end apart: 9, of which 9 were waited for; matrix products, arithmetic and copies ran while one was open for 6% of the time, Pallas kernels for 0%

profile of v1, /device:TPU:0, one launch (start us, length us, event | category | flops | bytes accessed | tf_op | source)
XLA Modules:
  0.0 884.2 jit_solution(16923370783971103217)
XLA Ops:
  13.7 29.7 %all-gather.5.cloned.1.call-done = bf16[1024,768]{1,0:T(8,128)(2,1)} async-done(((bf16[512,768]{1,0:T(8,128)(2,1)}), bf16[1024,768]{1,0:T(8,128)(2,1)}) %all-gather.5.cloned.1.call-update) | async-done | bytes 1572880 | tf_op jit(solution)/shard_map/all_gather | solution.py:71
  43.4 3.4 convolution_convert_fusion.3
  51.4 84.3 %while.29 = (s32[]{:T(128)}, bf16[2,512,6,64]{1,3,2,0:T(8,128)(2,1)}, f32[2,6,512]{2,1,0:T(8,128)S(1)}, s32[2]{0:T(128)S(1)}, s32[1024]{0:T(1024)S(1)}, /*index=...) while((s32[]{:T(128)}, ...), condition=%wide.region_7.8_spmd, body=%wide.region_4.7_spmd.sunk | while | flops 953901568 | bytes 133609992 | solution.py:106
  57.3 8.5 fusion.175
  65.7 15.3 %fusion.176 = (f32[6,512]{1,0:T(8,128)S(1)}, f32[6,512,1024]{2,1,0:T(8,128)S(1)}) fusion(f32[512,1024,6]{1,2,0:T(8,128)} %fusion.175, bf16[1024,6,64]{0,2,1:T(8,128)(2,1)S(1)} %get-tuple-element.419, bf16[1024,6,64]{0,2,1:T(8,128)(2,1)S(1)} %copy-done.8, s32[]{:T(128)S(6)} %select_n.59, pred[512,1024]{1,0:T(8,128)(4,1)S(1)} %broadcast_compare_fusion.4), kind=kOutput, calls=%fused_computation.146.clone.1 | convolution fusion | flops 415233024 | bytes 26882052 | tf_op jit(solution)/shard_map/while/body/eval_jaxpr/qhd,khd->hqk/dot_general | solution.py:84
  81.1 2.8 exponential_reduce_fusion.2
  85.8 6.7 fusion.178
  99.1 8.5 fusion.175
  107.6 15.3 %fusion.176 = (f32[6,512]{1,0:T(8,128)S(1)}, f32[6,512,1024]{2,1,0:T(8,128)S(1)}) fusion(f32[512,1024,6]{1,2,0:T(8,128)} %fusion.175, bf16[1024,6,64]{0,2,1:T(8,128)(2,1)S(1)} %get-tuple-element.419, bf16[1024,6,64]{0,2,1:T(8,128)(2,1)S(1)} %copy-done.8, s32[]{:T(128)S(6)} %select_n.59, pred[512,1024]{1,0:T(8,128)(4,1)S(1)} %broadcast_compare_fusion.4), kind=kOutput, calls=%fused_computation.146.clone.1 | convolution fusion | flops 415233024 | bytes 26882052 | tf_op jit(solution)/shard_map/while/body/eval_jaxpr/qhd,khd->hqk/dot_general | solution.py:84
  127.7 6.7 fusion.178
  142.3 42.7 %reduce-scatter.5.cloned.1.call-done = f32[512,768]{1,0:T(8,128)} async-done(((f32[1024,768]{1,0:T(8,128)}), f32[512,768]{1,0:T(8,128)}) %reduce-scatter.5.cloned.1.call-update) | async-done | bytes 1572880 | tf_op jit(solution)/shard_map/reduce_scatter | solution.py:108
  189.2 24.7 %all-gather.9.cloned.1.call-done = bf16[1024,768]{1,0:T(8,128)(2,1)} async-done(((bf16[512,768]{1,0:T(8,128)(2,1)}), bf16[1024,768]{1,0:T(8,128)(2,1)}) %all-gather.9.cloned.1.call-update) | async-done | bytes 1572880 | tf_op jit(solution)/shard_map/all_gather | solution.py:123
  213.8 7.5 fusion.101
  221.3 21.8 %all-gather.7.cloned.1.call-done = bf16[1024,768]{1,0:T(8,128)(2,1)} async-done(((bf16[512,768]{1,0:T(8,128)(2,1)}), bf16[1024,768]{1,0:T(8,128)(2,1)}) %all-gather.7.cloned.1.call-update) | async-done | bytes 1572880 | tf_op jit(solution)/shard_map/all_gather | solution.py:113
  243.1 9.7 %fusion.77 = (bf16[1024,1536]{1,0:T(8,128)(2,1)S(1)}, f32[1024,1536]{1,0:T(8,128)}) fusion(f32[1024,1536]{1,0:T(8,128)} %fusion.101, bf16[1024,768]{1,0:T(8,128)(2,1)} %all-gather.7.cloned.1.call-done, bf16[768,1536]{1,0:T(8,128)(2,1)S(1)} %copy-done), kind=kOutput, calls=%fused_computation.91 | convolution fusion | flops 2447376384 | bytes 19660800 | tf_op jit(solution)/shard_map/dot_general | solution.py:22
  254.5 3.7 convolution_convert_fusion
  258.3 8.4 convolution_convert_fusion.1
  266.8 17.7 %reduce-scatter.9.cloned.1.call-done = bf16[512,768]{1,0:T(8,128)(2,1)} async-done(((bf16[1024,768]{1,0:T(8,128)(2,1)}), bf16[512,768]{1,0:T(8,128)(2,1)}) %reduce-scatter.9.cloned.1.call-update) | async-done | bytes 786448 | tf_op jit(solution)/shard_map/reduce_scatter | solution.py:130
  287.0 25.7 %reduce-scatter.7.cloned.1.call-done = bf16[512,768]{1,0:T(8,128)(2,1)} async-done(((bf16[1024,768]{1,0:T(8,128)(2,1)}), bf16[512,768]{1,0:T(8,128)(2,1)}) %reduce-scatter.7.cloned.1.call-update) | async-done | bytes 786448 | tf_op jit(solution)/shard_map/reduce_scatter | solution.py:117
  312.7 2.9 fusion.97
  318.0 27.3 %all-gather.11.cloned.1.call-done = bf16[1024,768]{1,0:T(8,128)(2,1)} async-done(((bf16[512,768]{1,0:T(8,128)(2,1)}), bf16[1024,768]{1,0:T(8,128)(2,1)}) %all-gather.11.cloned.1.call-update) | async-done | bytes 1572880 | tf_op jit(solution)/shard_map/all_gather | solution.py:140
  345.4 3.1 convolution_convert_fusion.2
  349.4 214.1 %while.30 = (s32[]{:T(128)}, f32[1024,6,64]{0,2,1:T(8,128)}, f32[1024,6,64]{0,2,1:T(8,128)}, f32[6,16]{1,0:T(8,128)S(1)}, bf16[2,512,6,64]{1,3,2,0:T(8,128)(2,1)...) while((s32[]{:T(128)}, f32[1024,6,64]{0,2,1:T(8,128)}, ...), condition=%wide.region_17.18_spmd.clone, body=%wide.region_15.17_spmd.clone.sunk | while | flops 2483812096 | bytes 329461056 | solution.py:179
  356.1 6.4 fusion.191
  362.5 8.5 fusion.192
  371.0 15.7 %copy.43 = f32[512,1024,6]{1,0,2:T(8,128)} copy(f32[512,1024,6]{0,2,1:T(8,128)} %fusion.192) | data formatting | bytes 25165824 | tf_op jit(solution)/shard_map/while/body/eval_jaxpr/qkm,hm->hqk/dot_general | solution.py:88
  386.7 13.8 %multiply_reduce_fusion.3 = (f32[6,512]{1,0:T(8,128)S(1)}, f32[6,512,1024]{2,1,0:T(8,128)}) fusion(f32[6,512,1024]{2,1,0:T(8,128)} %fusion.191, f32[6,512]{1,0:T(8,128)S(1)} %dynamic-slice_bitcast_fusion.2, f32[512,1024,6]{1,0,2:T(8,128)} %copy.43, bf16[1024,6,64]{0,2,1:T(8,128)(2,1)S(1)} %get-tuple-element.465, ...), kind=kOutput, calls=%fused_computation.44.clone.1 | convolution fusion | flops 421524480 | bytes 39477252 | tf_op jit(solution)/shard_map/while/body/eval_jaxpr/qhd,khd->hqk/dot_general | solution.py:84
  400.5 9.1 %subtract_multiply_fusion.2 = f32[6,512,1024]{2,1,0:T(8,128)S(1)} fusion(f32[6,512,1024]{2,1,0:T(8,128)} %get-tuple-element.387, f32[6,512,1024]{2,1,0:T(8,128)} %fusion.191, f32[6,512]{1,0:T(8,128)S(1)} %get-tuple-element.388), kind=kLoop, calls=%fused_computation.43.clone.1 | loop fusion | flops 6291456 | bytes 37761024 | tf_op jit(solution)/shard_map/while/body/eval_jaxpr/mul | solution.py:155
  412.5 2.9 bitcast_add_fusion.7
  415.4 2.8 fusion.194
  418.2 3.5 bitcast_add_fusion.6
  421.8 16.0 %copy.44 = f32[6,512,1024]{1,0,2:T(8,128)} copy(f32[6,512,1024]{2,1,0:T(8,128)} %copy-done.2) | data formatting | bytes 25165824 | tf_op jit(solution)/shard_map/while/body/eval_jaxpr/mul | solution.py:155
  437.7 17.4 %fusion.193 = f32[6,16]{1,0:T(8,128)S(1)} fusion(f32[6,512,1024]{1,0,2:T(8,128)} %copy.44, s32[512,1024]{0,1:T(8,128)S(1)} %select_add_fusion.5, f32[6,16]{1,0:T(8,128)S(1)} %get-tuple-element.444, pred[]{:T(512)S(6)} %compare.3), kind=kOutput, calls=%fused_computation.69.clone.1 | convolution fusion | flops 310378688 | bytes 14680833 | tf_op jit(solution)/shard_map/while/body/eval_jaxpr/hqk,qkm->hm/dot_general | solution.py:156
  461.7 6.4 fusion.191
  468.1 8.5 fusion.192
  476.6 15.7 %copy.43 = f32[512,1024,6]{1,0,2:T(8,128)} copy(f32[512,1024,6]{0,2,1:T(8,128)} %fusion.192) | data formatting | bytes 25165824 | tf_op jit(solution)/shard_map/while/body/eval_jaxpr/qkm,hm->hqk/dot_general | solution.py:88
  492.3 13.8 %multiply_reduce_fusion.3 = (f32[6,512]{1,0:T(8,128)S(1)}, f32[6,512,1024]{2,1,0:T(8,128)}) fusion(f32[6,512,1024]{2,1,0:T(8,128)} %fusion.191, f32[6,512]{1,0:T(8,128)S(1)} %dynamic-slice_bitcast_fusion.2, f32[512,1024,6]{1,0,2:T(8,128)} %copy.43, bf16[1024,6,64]{0,2,1:T(8,128)(2,1)S(1)} %get-tuple-element.465, ...), kind=kOutput, calls=%fused_computation.44.clone.1 | convolution fusion | flops 421524480 | bytes 39477252 | tf_op jit(solution)/shard_map/while/body/eval_jaxpr/qhd,khd->hqk/dot_general | solution.py:84
  506.1 9.1 %subtract_multiply_fusion.2 = f32[6,512,1024]{2,1,0:T(8,128)S(1)} fusion(f32[6,512,1024]{2,1,0:T(8,128)} %get-tuple-element.387, f32[6,512,1024]{2,1,0:T(8,128)} %fusion.191, f32[6,512]{1,0:T(8,128)S(1)} %get-tuple-element.388), kind=kLoop, calls=%fused_computation.43.clone.1 | loop fusion | flops 6291456 | bytes 37761024 | tf_op jit(solution)/shard_map/while/body/eval_jaxpr/mul | solution.py:155
  518.1 5.0 bitcast_add_fusion.7
  523.1 2.8 fusion.194
  525.9 4.0 bitcast_add_fusion.6
  529.9 16.0 %copy.44 = f32[6,512,1024]{1,0,2:T(8,128)} copy(f32[6,512,1024]{2,1,0:T(8,128)} %copy-done.2) | data formatting | bytes 25165824 | tf_op jit(solution)/shard_map/while/body/eval_jaxpr/mul | solution.py:155
  545.9 17.4 %fusion.193 = f32[6,16]{1,0:T(8,128)S(1)} fusion(f32[6,512,1024]{1,0,2:T(8,128)} %copy.44, s32[512,1024]{0,1:T(8,128)S(1)} %select_add_fusion.5, f32[6,16]{1,0:T(8,128)S(1)} %get-tuple-element.444, pred[]{:T(512)S(6)} %compare.3), kind=kOutput, calls=%fused_computation.69.clone.1 | convolution fusion | flops 310378688 | bytes 14680833 | tf_op jit(solution)/shard_map/while/body/eval_jaxpr/hqk,qkm->hm/dot_general | solution.py:156
  571.9 7.3 fusion.108
  579.2 8.8 fusion.96
  601.8 5.0 all-reduce.2
  606.8 63.5 %all-reduce = (f32[768]{0:T(1024)}, f32[768]{0:T(1024)}, f32[6,16]{1,0:T(8,128)}) all-reduce(f32[768]{0:T(1024)S(1)} %get-tuple-element.234, f32[768]{0:T(1024)S(1)} %get-tuple-element.235, f32[6,16]{1,0:T(8,128)S(1)} %get-tuple-element.134), channel_id=1, replica_groups=mesh['dp'=16,'tensor'=2] {'dp'}, use_global_device_ids=true, to_apply=%region_23.24 | all-reduce | flops 1632 | bytes 13056 | tf_op jit(solution)/shard_map/psum | solution.py:204
  673.1 192.2 %all-reduce.5.cloned.1.call-done = (f32[768,384]{1,0:T(8,128)}, f32[768,384]{1,0:T(8,128)}, f32[768,384]{1,0:T(8,128)}, f32[384,768]{1,0:T(8,128)}, f32[768,1536]{1,0:T(8,128)}, /*index=5*/f32[1536,768]{1,0:T(8,128)}) async-done(((f32[768,384]{1,0:T(8,128)}, f32[768,384]{1,0:T(8,128)}, f32[768,384]{1,0:T(8,128)}, f32[384,768]{1,0:T(8,128)}, f32[768,1536]{1,0:T(8,128)}, /*index=5*/f32[1536,768]{1,0:T(8,128)}), ...) | async-done | bytes 14155792 | tf_op jit(solution)/shard_map/psum | solution.py:200
  (229 shorter events, 96.5 us)
Async XLA Ops:
  7.2 236.0 %copy-start = (bf16[768,1536]{1,0:T(8,128)(2,1)S(1)}, bf16[768,1536]{1,0:T(8,128)(2,1)}, u32[]{:S(2)}) copy-start(bf16[768,1536]{1,0:T(8,128)(2,1)} %param.25) | copy-start | bytes 7077892
  7.2 4.9 copy-start.11
  7.2 6.2 copy-start.51
  7.2 36.2 %all-gather.5.cloned.1.call-start = ((), (), s32[]{:S(2)}) async-start(), calls=%async_computation.4 | async-start | bytes 2359296 | tf_op jit(solution)/shard_map/all_gather | solution.py:71
  13.3 171.7 %reduce-scatter.5.cloned.1.call-start = ((), (), s32[]{:S(2)}) async-start(), calls=%async_computation.5 | async-start | bytes 4718592 | tf_op jit(solution)/shard_map/reduce_scatter | solution.py:108
  57.3 8.5 copy-start.8
  81.1 4.7 copy-start.3
  81.1 4.7 copy-start.5
  81.1 4.7 copy-start.20
  99.1 8.5 copy-start.8
  122.9 4.7 copy-start.3
  122.9 4.7 copy-start.5
  122.9 4.7 copy-start.20
  141.5 72.4 %all-gather.9.cloned.1.call-start = ((), (), s32[]{:S(2)}) async-start(), calls=%async_computation.8 | async-start | bytes 2359296 | tf_op jit(solution)/shard_map/all_gather | solution.py:123
  142.2 100.9 %all-gather.7.cloned.1.call-start = ((), (), s32[]{:S(2)}) async-start(), calls=%async_computation.6 | async-start | bytes 2359296 | tf_op jit(solution)/shard_map/all_gather | solution.py:113
  189.1 95.4 %reduce-scatter.9.cloned.1.call-start = ((), (), s32[]{:S(2)}) async-start(), calls=%async_computation.9 | async-start | bytes 2359296 | tf_op jit(solution)/shard_map/reduce_scatter | solution.py:130
  258.3 54.4 %reduce-scatter.7.cloned.1.call-start = ((), (), s32[]{:S(2)}) async-start(), calls=%async_computation.7 | async-start | bytes 2359296 | tf_op jit(solution)/shard_map/reduce_scatter | solution.py:117
  266.8 17.8 %copy-start.10 = (f32[512,768]{1,0:T(8,128)S(1)}, f32[512,768]{1,0:T(8,128)}, u32[]{:S(2)}) copy-start(f32[512,768]{1,0:T(8,128)} %copy-done.9) | copy-start | bytes 4718596
  266.8 78.6 %all-gather.11.cloned.1.call-start = ((), (), s32[]{:S(2)}) async-start(), calls=%async_computation.10 | async-start | bytes 2359296 | tf_op jit(solution)/shard_map/all_gather | solution.py:140
  287.0 29.8 %copy-start.17 = (bf16[512,768]{1,0:T(8,128)(2,1)S(1)}, bf16[512,768]{1,0:T(8,128)(2,1)}, u32[]{:S(2)}) copy-start(bf16[512,768]{1,0:T(8,128)(2,1)} %param.17) | copy-start | bytes 2359300
  315.7 29.7 %copy-start.29 = (bf16[384,768]{1,0:T(8,128)(2,1)S(1)}, bf16[384,768]{1,0:T(8,128)(2,1)}, u32[]{:S(2)}) copy-start(bf16[384,768]{1,0:T(8,128)(2,1)} %param.24) | copy-start | bytes 1769476
  315.7 32.8 %copy-start.41 = (f32[512]{0:T(512)}, f32[512]{0:T(512)S(1)}, u32[]{:S(2)}) copy-start(f32[512]{0:T(512)S(1)} %negate_multiply_fusion.1) | copy-start | bytes 6148
  318.0 280.1 %reduce-scatter.11.cloned.1.call-start = ((), (), s32[]{:S(2)}) async-start(), calls=%async_computation.11 | async-start | bytes 2359296 | tf_op jit(solution)/shard_map/reduce_scatter | solution.py:191
  352.1 4.0 copy-start.6
  352.1 4.0 copy-start.13
  400.5 11.8 %copy-start.4 = (f32[6,512,1024]{2,1,0:T(8,128)S(1)}, f32[6,512,1024]{2,1,0:T(8,128)}, u32[]{:S(2)}) copy-start(f32[6,512,1024]{2,1,0:T(8,128)} %get-tuple-element.387) | copy-start | bytes 37748740 | tf_op jit(solution)/shard_map/while
  400.5 11.9 %copy-start.14 = (bf16[1024,6,64]{0,2,1:T(8,128)(2,1)S(1)}, bf16[1024,6,64]{0,2,1:T(8,128)(2,1)}, u32[]{:S(2)}) copy-start(bf16[1024,6,64]{0,2,1:T(8,128)(2,1)} %get-tuple-element.468) | copy-start | bytes 2359300 | tf_op jit(solution)/shard_map/while
  412.5 5.8 copy-start.2
  457.7 4.0 copy-start.6
  457.7 4.0 copy-start.13
  506.1 11.8 %copy-start.4 = (f32[6,512,1024]{2,1,0:T(8,128)S(1)}, f32[6,512,1024]{2,1,0:T(8,128)}, u32[]{:S(2)}) copy-start(f32[6,512,1024]{2,1,0:T(8,128)} %get-tuple-element.387) | copy-start | bytes 37748740 | tf_op jit(solution)/shard_map/while
  506.1 11.9 %copy-start.14 = (bf16[1024,6,64]{0,2,1:T(8,128)(2,1)S(1)}, bf16[1024,6,64]{0,2,1:T(8,128)(2,1)}, u32[]{:S(2)}) copy-start(bf16[1024,6,64]{0,2,1:T(8,128)(2,1)} %get-tuple-element.468) | copy-start | bytes 2359300 | tf_op jit(solution)/shard_map/while
  518.0 7.9 copy-start.2
  571.9 293.4 %all-reduce.5.cloned.1.call-start = ((), (), s32[]{:S(2)}) async-start(), calls=%async_computation.12 | async-start | bytes 28311552 | tf_op jit(solution)/shard_map/psum | solution.py:200
  571.9 7.3 copy-start.49
  579.2 8.8 copy-start.24
  579.2 8.8 copy-start.50
  595.9 3.8 copy-start.44
  596.0 3.8 copy-start.40
  596.0 5.8 copy-start.45
  596.0 74.3 %copy-start.16 = (f32[512,768]{1,0:T(8,128)S(1)}, f32[512,768]{1,0:T(8,128)}, u32[]{:S(2)}) copy-start(f32[512,768]{1,0:T(8,128)} %copy-done.15) | copy-start | bytes 4718596
  596.0 74.3 %copy-start.18 = (bf16[512,768]{1,0:T(8,128)(2,1)S(1)}, bf16[512,768]{1,0:T(8,128)(2,1)}, u32[]{:S(2)}) copy-start(bf16[512,768]{1,0:T(8,128)(2,1)} %param.17) | copy-start | bytes 2359300
  596.0 74.3 %copy-start.42 = (f32[512]{0:T(512)S(1)}, f32[512]{0:T(512)}, u32[]{:S(2)}) copy-start(f32[512]{0:T(512)} %copy-done.41) | copy-start | bytes 6148
  865.3 3.5 copy-start.26
  865.3 4.5 copy-start.25
  867.8 3.6 copy-start.19
  869.8 3.8 slice-start
  873.9 3.4 copy-start.1
  (25 other events, 42.4 us)
Sparse Core Ops, SparseCore 0:
  13.4 29.8 all-gather.4
  141.6 43.3 reduce-scatter.4
  186.6 27.2 all-gather.8
  215.9 27.1 all-gather.6
  258.4 26.0 reduce-scatter.8
  286.6 26.0 reduce-scatter.6
  318.1 27.2 all-gather.10
  572.0 26.0 reduce-scatter.10
  604.4 260.8 all-reduce.4
